TPU v7x, 1024 devices: a whole 4x8x16 slice. The times are simulated.
1024 devices in a mesh: dom: 64 (over y, z_lo), orb: 16 (over x, z_hi, core).
Axes of the slice: x: 4, y: 8, z: 16 (z_hi: 2, z_lo: 8; z = z_hi * 8 + z_lo), core: 2. Of those that a mesh axis runs over, the one named last changes fastest.
Arguments:
- orbitals: bfloat16 [150528, 1024], P('dom', 'orb'), may hold values from -16 to 16
- potential: float32 [150528], P('dom'), may hold values from 0.5 to 2
- cell_hamiltonian: bfloat16 [512, 343, 343], P('dom'), may hold values from -2 to 2, as said below
- connectivity: int32 [512, 343], P('dom'), may hold values from 0 to 2400, as said below
- face_nodes: int32 [3136], P('dom'), may hold values from 0 to 2351, as said below
Outputs:
- residual: float32 [150528, 1024], P(('dom', 'orb'))
- projected: bfloat16 [1024, 1024], replicated
Inputs may be any that keep to these rules, and one draw needn't show every extreme that they name: `connectivity`: cell c of a domain is its c-th layer of cells; each row lists the cell's 343 nodes in the domain's local numbering, where a number 2352 + p stands for entry p of the next domain's face_nodes list. Every local node of a domain belongs to some cell of it, and neighbouring cells of a domain share a face of 49 nodes. `face_nodes`: each domain's 49 entries are distinct local node numbers of that domain: the nodes that the previous domain's last cell shares with it, in the order of that cell's numbers 2352 + p. `cell_hamiltonian`: each cell's matrix is symmetric.
All inputs are finite; a program needn't handle non-finite values.
Results may differ from a plain program's by a relative error of at most 0.0096.
Values may be sent and summed in bfloat16 or wider, within the bound.
A program may use at most 32 MiB of HBM per device.

v0:
```python
import jax
import jax.numpy as jnp
from jax import lax
from jax.sharding import PartitionSpec as P

DEGREE = 4


filter_center = 1.5
filter_half = 2.0


def from_behind(block, axis, distance):
    devices = range(lax.axis_size(axis))
    route = [(i - distance, i) for i in devices if i - distance in devices]
    return lax.ppermute(block, axis, route)


def apply_hamiltonian(values, potential, cell_hamiltonian, connectivity, face_nodes):
    node_count = values.shape[1]
    face_vals = jnp.take(values, face_nodes, axis=1)
    ghosts = from_behind(face_vals, "dom", -1)
    extended = jnp.concatenate([values, ghosts], axis=1)
    cell_values = jnp.take(extended, connectivity, axis=1)
    products = jnp.einsum(
        "kij,okj->oki", cell_hamiltonian, cell_values, preferred_element_type=jnp.float32
    )
    summed = (
        jnp.zeros((values.shape[0], extended.shape[1]), jnp.float32)
        .at[:, connectivity]
        .add(products)
    )
    returned = from_behind(summed[:, node_count:], "dom", 1)
    assembled = summed[:, :node_count].at[:, face_nodes].add(returned)
    return assembled + potential[None, :] * values.astype(jnp.float32)


def body(orbitals, potential, cell_hamiltonian, connectivity, face_nodes):
    previous = orbitals.T
    image = apply_hamiltonian(previous, potential, cell_hamiltonian, connectivity, face_nodes)
    current = ((image - filter_center * previous.astype(jnp.float32)) / filter_half).astype(
        jnp.bfloat16
    )
    for step in range(DEGREE - 1):
        image = apply_hamiltonian(current, potential, cell_hamiltonian, connectivity, face_nodes)
        following_iter = (
            2.0 * (image - filter_center * current.astype(jnp.float32)) / filter_half
            - previous.astype(jnp.float32)
        ).astype(jnp.bfloat16)
        previous, current = (current, following_iter)
    image = apply_hamiltonian(
        current, potential, cell_hamiltonian, connectivity, face_nodes
    ).astype(jnp.bfloat16)
    node_rows, image_rows = (
        lax.all_to_all(current.T, "orb", split_axis=0, concat_axis=1, tiled=True),
        lax.all_to_all(image.T, "orb", split_axis=0, concat_axis=1, tiled=True),
    )
    node_total = node_rows.shape[0] * lax.axis_size("orb") * lax.axis_size("dom")
    inverse_nodes = 1.0 / node_total
    share = lax.psum_scatter(
        jnp.einsum("ri,rj->ij", node_rows, image_rows, preferred_element_type=jnp.float32)
        * inverse_nodes,
        "orb",
        scatter_dimension=0,
        tiled=True,
    )
    share = lax.psum(share, "dom")
    projected = lax.all_gather(share.astype(jnp.bfloat16), "orb", axis=0, tiled=True)
    residual = image_rows.astype(jnp.float32) - jnp.dot(
        node_rows, projected, preferred_element_type=jnp.float32
    )
    return (residual, projected)


def solution(mesh):
    return jax.shard_map(
        body,
        mesh=mesh,
        in_specs=(P("dom", "orb"), P("dom"), P("dom", None, None), P("dom", None), P("dom")),
        out_specs=(P(("dom", "orb"), None), P()),
        check_vma=False,
    )
```

profile of v0, /device:TPU:1, one launch (start us, length us, event | category | flops | bytes accessed | tf_op | source)
XLA Modules:
  0.0 1091.6 jit_solution(3182789114470864673)
XLA Ops:
  8.6 1.3 copy.49
  13.5 3.1 collective-permute-done
  16.7 6.6 gather_fusion.1
  23.3 1.4 copy.50
  26.0 1.5 copy.81
  27.5 2.5 reshape.241
  30.1 18.4 %scatter_custom_fusion = f32[64,2401]{0,1:T(8,128)} fusion(s32[2744]{0:T(1024)S(1)} %reshape.167, f32[2744,64]{1,0:T(8,128)} %reshape.241, f32[]{:T(128)} %constant.23.clone.1), kind=kCustom, calls=%fused_computation.70 | custom fusion | flops 175616 | bytes 615168 | tf_op jit(solution)/shard_map/scatter-add | solution.py:31
  49.2 4.0 collective-permute-start.1
  53.2 2.7 fusion.2
  55.9 3.1 scatter_custom_fusion.1
  58.9 2.3 fusion.5
  61.2 1.7 gather_fusion.2
  64.3 3.8 collective-permute-done.2
  69.3 6.6 gather_fusion.3
  75.9 1.4 copy.55
  78.6 1.5 copy.82
  80.2 2.5 reshape.242
  82.7 18.4 %scatter_custom_fusion.2 = f32[64,2401]{0,1:T(8,128)} fusion(s32[2744]{0:T(1024)S(1)} %reshape.167, f32[2744,64]{1,0:T(8,128)} %reshape.242, f32[]{:T(128)} %constant.23.clone.1), kind=kCustom, calls=%fused_computation.68 | custom fusion | flops 175616 | bytes 615168 | tf_op jit(solution)/shard_map/scatter-add | solution.py:31
  101.8 5.4 collective-permute-start.3
  107.2 2.9 fusion.7
  110.1 3.1 scatter_custom_fusion.3
  113.1 1.7 fusion.6
  116.8 3.8 collective-permute-done.4
  120.7 6.6 gather_fusion.5
  127.3 2.1 copy.60
  129.4 1.5 reshape.228
  131.0 1.6 convolution_bitcast_fusion.2
  132.6 2.7 copy.83
  135.3 2.5 reshape.243
  137.8 18.4 %scatter_custom_fusion.4 = f32[64,2401]{0,1:T(8,128)} fusion(s32[2744]{0:T(1024)S(1)} %reshape.167, f32[2744,64]{1,0:T(8,128)} %reshape.243, f32[]{:T(128)} %constant.23.clone.1), kind=kCustom, calls=%fused_computation.66 | custom fusion | flops 175616 | bytes 615168 | tf_op jit(solution)/shard_map/scatter-add | solution.py:31
  156.9 4.7 collective-permute-start.5
  161.6 2.7 fusion.10
  164.3 3.1 scatter_custom_fusion.5
  167.4 2.5 fusion.9
  170.0 1.7 gather_fusion.6
  173.1 3.2 collective-permute-done.6
  177.4 6.6 gather_fusion.7
  184.0 2.1 copy.65
  186.1 1.5 reshape.234
  187.7 1.6 convolution_bitcast_fusion.1
  189.3 2.7 copy.84
  192.0 2.5 reshape.244
  194.5 18.4 %scatter_custom_fusion.6 = f32[64,2401]{0,1:T(8,128)} fusion(s32[2744]{0:T(1024)S(1)} %reshape.167, f32[2744,64]{1,0:T(8,128)} %reshape.244, f32[]{:T(128)} %constant.23.clone.1), kind=kCustom, calls=%fused_computation.64 | custom fusion | flops 175616 | bytes 615168 | tf_op jit(solution)/shard_map/scatter-add | solution.py:31
  213.6 11.0 %collective-permute-start.7 = (f32[64,49]{0,1:T(8,128)S(1)}, f32[64,49]{0,1:T(8,128)S(1)}, u32[]{:S(2)}, u32[]{:S(2)}) collective-permute-start(f32[64,49]{0,1:T(8,128)S(1)} %slice.67), channel_id=1, source_target_pairs={{0,16},{16,32},{32,48},{48,64},{64,80},{80,96},{96,112},{112,128},... | collective-permute-start | bytes 37640 | tf_op jit(solution)/shard_map/ppermute | solution.py:16
  224.6 2.9 fusion
  227.5 3.1 scatter_custom_fusion.7
  230.5 1.7 fusion.12
  235.5 19.2 %all-to-all-start.1 = ((bf16[16,147,64]{1,2,0:T(8,128)(2,1)}), bf16[16,147,64]{1,2,0:T(8,128)(2,1)}, u32[]{:S(2)}, u32[]{:S(2)}) async-start(bf16[16,147,64]{1,2,0:T(8,128)(2,1)} %copy.79), calls=%async_computation.1 | async-start | bytes 1048576 | tf_op jit(solution)/shard_map/all_to_all | solution.py:55
  256.0 5.8 gather_fusion.9
  262.9 1.5 reshape.240
  264.4 1.6 convolution_bitcast_fusion
  266.1 1.6 copy.85
  268.8 18.4 %scatter_custom_fusion.8 = f32[64,2401]{0,1:T(8,128)} fusion(s32[2744]{0:T(1024)S(1)} %reshape.167, f32[2744,64]{1,0:T(8,128)} %reshape.245, f32[]{:T(128)} %constant.23.clone.1), kind=kCustom, calls=%fused_computation.62 | custom fusion | flops 175616 | bytes 615168 | tf_op jit(solution)/shard_map/scatter-add | solution.py:31
  288.0 4.3 collective-permute-start.9
  292.2 2.7 slice_add_fusion
  294.9 3.1 scatter_custom_fusion.9
  298.0 1.3 convert_bitcast_fusion
  299.9 33.0 %all_to_all.38 = bf16[16,147,64]{1,2,0:T(8,128)(2,1)S(1)} all-to-all(bf16[16,147,64]{1,2,0:T(8,128)(2,1)S(1)} %copy.76), channel_id=1, replica_groups=mesh['dom'=64,'orb'=16] {'orb'}, dimensions={0} | all-to-all | bytes 602112 | tf_op jit(solution)/shard_map/all_to_all | solution.py:56
  332.8 3.7 convolution_multiply_fusion
  336.6 196.6 %reduce-scatter.2.cloned.1.call-done = f32[64,1024]{1,0:T(8,128)} async-done(((f32[1024,1024]{1,0:T(8,128)}), f32[64,1024]{1,0:T(8,128)}) %reduce-scatter.2.cloned.1.call-update) | async-done | bytes 262160 | tf_op jit(solution)/shard_map/reduce_scatter | solution.py:60
  533.2 396.7 %all-reduce.1 = bf16[64,1024]{1,0:T(8,128)(2,1)} all-reduce(f32[64,1024]{1,0:T(8,128)} %reduce-scatter.2.cloned.1.call-done), channel_id=1, replica_groups=mesh['dom'=64,'orb'=16] {'dom'}, use_global_device_ids=true, to_apply=%region_11.14 | all-reduce | flops 65536 | bytes 393216 | tf_op jit(solution)/shard_map/psum | solution.py:67
  930.1 150.2 %all-gather.2.cloned.1.call-done = bf16[1024,1024]{1,0:T(8,128)(2,1)} async-done(((bf16[64,1024]{1,0:T(8,128)(2,1)}), bf16[1024,1024]{1,0:T(8,128)(2,1)}) %all-gather.2.cloned.1.call-update) | async-done | bytes 2097168 | tf_op jit(solution)/shard_map/all_gather | solution.py:68
  1080.2 3.2 convolution_subtract_fusion
  1083.5 1.3 copy.125
  (67 shorter events, 26.4 us)
Async XLA Ops:
  7.2 18.1 %copy-start = (bf16[8,343,343]{2,0,1:T(8,128)(2,1)S(1)}, bf16[8,343,343]{2,0,1:T(8,128)(2,1)}, u32[]{:S(2)}) copy-start(bf16[8,343,343]{2,0,1:T(8,128)(2,1)} %param.11) | copy-start | bytes 5647156
  10.7 5.9 collective-permute-start
  30.1 23.1 %copy-start.4 = (f32[2352]{0:T(1024)S(1)}, f32[2352]{0:T(1024)}, u32[]{:S(2)}) copy-start(f32[2352]{0:T(1024)} %param.10) | copy-start | bytes 28228
  49.2 6.7 collective-permute-start.1
  63.0 5.1 collective-permute-start.2
  101.8 8.2 collective-permute-start.3
  115.5 5.1 collective-permute-start.4
  156.9 7.4 collective-permute-start.5
  171.8 4.5 collective-permute-start.6
  213.6 13.9 %collective-permute-start.7 = (f32[64,49]{0,1:T(8,128)S(1)}, f32[64,49]{0,1:T(8,128)S(1)}, u32[]{:S(2)}, u32[]{:S(2)}) collective-permute-start(f32[64,49]{0,1:T(8,128)S(1)} %slice.67), channel_id=1, source_target_pairs={{0,16},{16,32},{32,48},{48,64},{64,80},{80,96},{96,112},{112,128},... | collective-permute-start | bytes 37640 | tf_op jit(solution)/shard_map/ppermute | solution.py:16
  232.2 22.6 %copy-start.1 = (bf16[64,2352]{0,1:T(8,128)(2,1)}, bf16[64,2352]{0,1:T(8,128)(2,1)S(1)}, u32[]{:S(2)}) copy-start(bf16[64,2352]{0,1:T(8,128)(2,1)S(1)} %fusion.12) | copy-start | bytes 903172
  232.9 21.9 %collective-permute-start.8 = (bf16[64,49]{0,1:T(8,128)(2,1)S(1)}, bf16[64,49]{0,1:T(8,128)(2,1)S(1)}, u32[]{:S(2)}, u32[]{:S(2)}) collective-permute-start(bf16[64,49]{0,1:T(8,128)(2,1)S(1)} %select_bitcast_fusion.5), channel_id=1, source_target_pairs={{16,0},{32,16},{48,32},{64,48},{80,64},{96,80},{112,96},{128,112},... | collective-permute-start | bytes 18824 | tf_op jit(solution)/shard_map/ppermute | solution.py:16
  235.5 64.3 %all-to-all-start.1 = ((bf16[16,147,64]{1,2,0:T(8,128)(2,1)}), bf16[16,147,64]{1,2,0:T(8,128)(2,1)}, u32[]{:S(2)}, u32[]{:S(2)}) async-start(bf16[16,147,64]{1,2,0:T(8,128)(2,1)} %copy.79), calls=%async_computation.1 | async-start | bytes 1048576 | tf_op jit(solution)/shard_map/all_to_all | solution.py:55
  254.8 278.4 %reduce-scatter.2.cloned.1.call-start = ((), (), s32[]{:S(2)}) async-start(), calls=%async_computation.3 | async-start | bytes 4456448 | tf_op jit(solution)/shard_map/reduce_scatter | solution.py:60
  268.8 23.4 %copy-start.2 = (bf16[64,2352]{0,1:T(8,128)(2,1)S(1)}, bf16[64,2352]{0,1:T(8,128)(2,1)}, u32[]{:S(2)}) copy-start(bf16[64,2352]{0,1:T(8,128)(2,1)} %copy-done.1) | copy-start | bytes 903172
  288.0 7.0 collective-permute-start.9
  336.6 743.6 %all-gather.2.cloned.1.call-start = ((), (), s32[]{:S(2)}) async-start(), calls=%async_computation.4 | async-start | bytes 2228224 | tf_op jit(solution)/shard_map/all_gather | solution.py:68
  1080.2 3.2 copy-start.3
Sparse Core Ops, SparseCore 0:
  336.7 196.4 reduce-scatter.1
  930.0 150.1 all-gather.1
where the time goes:
time: 1090 us
  blocking collectives  430 us (39%)
  waiting for transfers between devices  361 us (33%)
  other arithmetic  138 us (13%)
  local copies, waits for them, and re-layouts  80.6 us (7%)
  starting transfers between devices  55.1 us (5%)
  between operations  14.4 us (1%)
  matrix products  13.4 us (1%)
    psum x1, blocking collectives, body(): share = lax.psum(share, 'dom')  397 us
    reduce_scatter x1, waiting for transfers between devices, body(): lax.psum_scatter(jnp.einsum('ri,rj->ij', node_rows, image_rows, preferred...  197 us
    all_gather x1, waiting for transfers between devices, body(): lax.all_gather(share.astype(jnp.bfloat16), 'orb', axis=0, tiled=True)  150 us
    scatter-add x5, other arithmetic, apply_hamiltonian(): summed = jnp.zeros((values.shape[0], extended.shape[1]), jnp.float32).at[...  91.8 us
    gather x15, local copies, waits for them, and re-layouts, apply_hamiltonian(): cell_values = jnp.take(extended, connectivity, axis=1)  45.6 us
    ppermute x10, starting transfers between devices, from_behind(): return lax.ppermute(block, axis, route)  35.7 us
    all_to_all x1, blocking collectives, body(): lax.all_to_all(image.T, 'orb', split_axis=0, concat_axis=1, tiled=True)  33 us
  transfers between devices with their start and end apart: 13, of which 6 were waited for; matrix products, arithmetic and copies ran while one was open for 5% of the time, Pallas kernels for 0%

commit v1 on v0

v1 whole, which is shorter than its diff:
```python
import functools

import jax
import jax.numpy as jnp
from jax import lax
from jax.experimental import pallas as pl
from jax.experimental.pallas import tpu as pltpu
from jax.sharding import PartitionSpec as P

DEGREE = 4
MESH = pl.DeviceIdType.MESH
F32 = jnp.float32
BF16 = jnp.bfloat16

filter_center = 1.5
filter_half = 2.0

SIDE = 64
STRIDE = 320
SPAN = STRIDE + SIDE


def prefix_tables(n):
    before = lax.broadcasted_iota(jnp.int32, (n, n), 0) < lax.broadcasted_iota(jnp.int32, (n, n), 1)
    after = lax.broadcasted_iota(jnp.int32, (n, n), 0) > lax.broadcasted_iota(jnp.int32, (n, n), 1)
    return before.astype(F32).astype(BF16), after.astype(F32).astype(BF16)


def dot(a, b):
    return jnp.dot(a, b, preferred_element_type=F32)


def equal(a, b):
    return (a == b).astype(F32)


def filter_kernel(
    sizes,
    nodes_ref,
    mats_ref,
    conn_ref,
    conn_col_ref,
    face_ref,
    face_col_ref,
    out_ref,
    values,
    cellmats,
    total,
    pots,
    ids_col,
    ids_row,
    both,
    ghosts,
    behind,
    behind_mat,
    send_sem,
    recv_sem,
    mat_sem,
):
    cells, npc, owned, share, blocks = sizes
    dom = lax.axis_index("dom")
    domains = lax.axis_size("dom")
    nxt = lax.rem(dom + 1, domains)
    prv = lax.rem(dom + domains - 1, domains)
    barrier = pltpu.get_barrier_semaphore()
    for other in (prv, nxt):
        pl.semaphore_signal(barrier, inc=1, device_id={"dom": other}, device_id_type=MESH)

    rows = [conn_ref[c : c + 1, :] for c in range(cells)]
    cols = [conn_col_ref[:, c : c + 1] for c in range(cells)]
    face_row, face_col = face_ref[...], face_col_ref[...]
    faces = face_row.shape[1]

    low = [equal(cols[c], rows[c + 1]) for c in range(cells - 1)]
    high = [equal(cols[c + 1], rows[c]) for c in range(cells - 1)]
    first_row = equal(face_col, rows[0])
    first_col = equal(cols[0], face_row)
    bottom_row = [jnp.sum(first_row, axis=0, keepdims=True)]
    bottom_row += [jnp.sum(low[c], axis=0, keepdims=True) for c in range(cells - 1)]
    bottom_col = [jnp.sum(first_col, axis=1, keepdims=True)]
    bottom_col += [jnp.sum(high[c], axis=1, keepdims=True) for c in range(cells - 1)]
    top_row = [jnp.sum(high[c], axis=0, keepdims=True) for c in range(cells - 1)]
    top_row += [(rows[-1] >= owned).astype(F32)]
    top_col = [jnp.sum(low[c], axis=1, keepdims=True) for c in range(cells - 1)]
    top_col += [(cols[-1] >= owned).astype(F32)]

    before, after = prefix_tables(npc)
    inner_row = [1.0 - bottom_row[c] - top_row[c] for c in range(cells)]
    inner_col = [1.0 - bottom_col[c] - top_col[c] for c in range(cells)]
    stacked_row = jnp.concatenate(bottom_row + inner_row, axis=0).astype(BF16)
    stacked_col = jnp.concatenate(bottom_col + inner_col, axis=1).astype(BF16)
    rank_row = dot(stacked_row, before)
    rank_col = dot(after, stacked_col)
    place_row = lax.broadcasted_iota(jnp.int32, (faces, 1), 0).astype(F32)
    place_col = lax.broadcasted_iota(jnp.int32, (1, faces), 1).astype(F32)
    low_row = [jnp.sum(first_row * place_row, axis=0, keepdims=True)]
    low_row += [rank_row[c : c + 1] for c in range(1, cells)]
    low_col = [jnp.sum(first_col * place_col, axis=1, keepdims=True)]
    low_col += [rank_col[:, c : c + 1] for c in range(1, cells)]
    high_row = [jnp.sum(high[c] * low_col[c + 1], axis=0, keepdims=True) for c in range(cells - 1)]
    high_row += [(rows[-1] - owned).astype(F32)]
    high_col = [jnp.sum(low[c] * low_row[c + 1], axis=1, keepdims=True) for c in range(cells - 1)]
    high_col += [(cols[-1] - owned).astype(F32)]

    def slots(bottom, top, low_rank, high_rank, inner_rank):
        inner = SIDE + inner_rank
        return jnp.where(bottom > 0.5, low_rank, jnp.where(top > 0.5, STRIDE + high_rank, inner)).astype(
            jnp.int32
        )

    def spread_of(c):
        slot_row = slots(
            bottom_row[c], top_row[c], low_row[c], high_row[c], rank_row[cells + c : cells + c + 1]
        )
        slot_col = slots(
            bottom_col[c], top_col[c], low_col[c], high_col[c], rank_col[:, cells + c : cells + c + 1]
        )
        down = equal(lax.broadcasted_iota(jnp.int32, (SPAN, npc), 0), slot_row)
        across = equal(slot_col, lax.broadcasted_iota(jnp.int32, (npc, SPAN), 1))
        return down, across

    order = [cells - 1] + list(range(cells - 1))
    for c in order:
        down, across = spread_of(c)
        named = rows[c].astype(F32) + 1.0
        ids_col[c] = (jnp.sum(down * named, axis=1, keepdims=True) - 1.0).astype(jnp.int32)
        named = cols[c].astype(F32) + 1.0
        ids_row[c] = (jnp.sum(across * named, axis=0, keepdims=True) - 1.0).astype(jnp.int32)
        half = dot(down.astype(BF16), mats_ref[c]).astype(BF16)
        cellmats[c] = dot(half, across.astype(BF16)).astype(BF16)

    pl.semaphore_wait(barrier, 2)
    mat_copy = pltpu.make_async_remote_copy(
        src_ref=cellmats.at[cells - 1, pl.ds(STRIDE, SIDE)],
        dst_ref=behind_mat,
        send_sem=mat_sem.at[0],
        recv_sem=mat_sem.at[1],
        device_id={"dom": nxt},
        device_id_type=MESH,
    )
    mat_copy.start()

    width = values.shape[2]

    def take(c, carry):
        pick = equal(
            ids_col[c, pl.ds(0, STRIDE), :], lax.broadcasted_iota(jnp.int32, (STRIDE, owned), 1)
        )
        found = dot(pick.astype(BF16), nodes_ref[...])
        start = pl.multiple_of(c * STRIDE, STRIDE)
        values[0, pl.ds(start, STRIDE), :] = found[:, :width].astype(BF16)
        pot = found[:, width : width + 1] + found[:, width + 1 : width + 2] + found[:, width + 2 : width + 3]
        pots[pl.ds(start, STRIDE), :] = jnp.broadcast_to(pot, (STRIDE, width))
        return carry

    lax.fori_loop(0, cells, take, 0)

    end = cells * STRIDE
    has_next = (dom < domains - 1).astype(F32)
    has_prev = (dom > 0).astype(F32)
    copies = []
    for step in range(DEGREE + 1):
        back = pltpu.make_async_remote_copy(
            src_ref=values.at[step, pl.ds(0, SIDE)],
            dst_ref=ghosts.at[step],
            send_sem=send_sem.at[step, 0],
            recv_sem=recv_sem.at[step, 0],
            device_id={"dom": prv},
            device_id_type=MESH,
        )
        ahead = pltpu.make_async_remote_copy(
            src_ref=values.at[step, pl.ds(end - STRIDE, STRIDE)],
            dst_ref=behind.at[step],
            send_sem=send_sem.at[step, 1],
            recv_sem=recv_sem.at[step, 1],
            device_id={"dom": nxt},
            device_id_type=MESH,
        )
        back.start()
        ahead.start()
        copies += [back, ahead]
        total[...] = jnp.zeros_like(total)
        for c in range(cells - 1):
            span = pl.ds(c * STRIDE, SPAN)
            total[span, :] += dot(cellmats[c], values[step, span, :])
        back.wait_recv()
        values[step, pl.ds(end, SIDE), :] = (ghosts[step].astype(F32) * has_next).astype(BF16)
        span = pl.ds(end - STRIDE, SPAN)
        total[span, :] += dot(cellmats[cells - 1], values[step, span, :])
        if step == 0:
            mat_copy.wait_recv()
        ahead.wait_recv()
        shared = dot(behind_mat[:, :STRIDE], behind[step]) + dot(
            behind_mat[:, STRIDE:], values[step, pl.ds(0, SIDE), :]
        )
        total[pl.ds(0, SIDE), :] += shared * has_prev
        own = pl.ds(0, end)
        current = values[step, own, :].astype(F32)
        image = total[own, :] + pots[...] * current
        if step == 0:
            values[1, own, :] = ((image - filter_center * current) / filter_half).astype(BF16)
        elif step < DEGREE:
            previous = values[step - 1, own, :].astype(F32)
            scaled = 2.0 * (image - filter_center * current) / filter_half
            values[step + 1, own, :] = (scaled - previous).astype(BF16)
        else:
            both[:, :width] = values[step, own, :]
            both[:, width:] = image.astype(BF16)

    def give(b, carry):
        part = out_ref.shape[1]
        row = lax.broadcasted_iota(jnp.int32, (part, STRIDE), 0)
        target = jnp.where(row < share, row + b * share, -2)
        found = jnp.zeros((part, 2 * width), F32)
        for c in range(cells):
            pick = equal(ids_row[c, :, pl.ds(0, STRIDE)], target)
            found += dot(pick.astype(BF16), both[pl.ds(c * STRIDE, STRIDE), :])
        out_ref[b] = found.astype(BF16)
        return carry

    lax.fori_loop(0, blocks, give, 0)
    mat_copy.wait_send()
    for copy in copies:
        copy.wait_send()


BLOCK = 256


def project_kernel(
    sizes,
    rows_ref,
    residual_ref,
    projected_ref,
    left,
    right,
    packed,
    from_core,
    for_x,
    from_x,
    for_y,
    from_y,
    for_z,
    from_z,
    final,
    gathered,
    core_sem,
    x_sem,
    y_sem,
    z_sem,
    zg_sem,
    yg_sem,
    xg_sem,
    cg_sem,
):
    share, inverse = sizes
    dom, orb = lax.axis_index("dom"), lax.axis_index("orb")
    y, z_lo = dom // 8, lax.rem(dom, 8)
    x, z_hi, core = orb // 4, lax.rem(orb // 2, 2), lax.rem(orb, 2)
    z = z_hi * 8 + z_lo

    def at_core():
        return {"dom": dom, "orb": orb + 1 - 2 * core}

    def at_x(k):
        return {"dom": dom, "orb": lax.rem(x + k, 4) * 4 + z_hi * 2 + core}

    def at_y(k):
        return {"dom": lax.rem(y + k, 8) * 8 + z_lo, "orb": orb}

    def at_z(k):
        there = lax.rem(z + k, 16)
        return {"dom": y * 8 + lax.rem(there, 8), "orb": x * 4 + (there // 8) * 2 + core}

    barrier = pltpu.get_barrier_semaphore()

    def greet(peer):
        pl.semaphore_signal(barrier, inc=1, device_id=peer, device_id_type=MESH)

    greet(at_core())
    for k in range(1, 4):
        greet(at_x(k))
    for k in range(1, 8):
        greet(at_y(k))
    for k in range(1, 16):
        greet(at_z(k))

    def copy(src, dst, sems, k, peer):
        return pltpu.make_async_remote_copy(
            src_ref=src,
            dst_ref=dst,
            send_sem=sems.at[0, k],
            recv_sem=sems.at[1, k],
            device_id=peer,
            device_id_type=MESH,
        )

    blocks, part, lanes = rows_ref.shape
    lane = lax.broadcasted_iota(jnp.int32, (part, lanes), 1)
    for m in range(blocks // 2):
        a, b = rows_ref[2 * m].astype(F32), rows_ref[2 * m + 1].astype(F32)
        cut = pl.ds(m * lanes, lanes)
        left[:, cut] = jnp.where(lane < lanes // 2, a, pltpu.roll(b, lanes // 2, 1)).astype(BF16)
        right[:, cut] = jnp.where(lane < lanes // 2, pltpu.roll(a, lanes // 2, 1), b).astype(BF16)

    count = left.shape[1] // BLOCK
    pairs = [(i, j) for i in range(count) for j in range(i, count)]
    for p, (i, j) in enumerate(pairs):
        block = lax.dot_general(
            left[:, i * BLOCK : (i + 1) * BLOCK],
            right[:, j * BLOCK : (j + 1) * BLOCK],
            (((0,), (0,)), ((), ())),
            preferred_element_type=F32,
        ).astype(BF16)
        packed[pl.ds((2 * p) * BLOCK, BLOCK), :] = block[:, :128]
        packed[pl.ds((2 * p + 1) * BLOCK, BLOCK), :] = block[:, 128:]
    size = packed.shape[0]
    n2, n8, n64, n1024 = size // 2, size // 8, size // 64, size // 1024

    pl.semaphore_wait(barrier, 26)
    waits = []
    step = copy(
        packed.at[pl.ds(pl.multiple_of((1 - core) * n2, n2), n2)], from_core, core_sem, 0, at_core()
    )
    step.start()
    step.wait_recv()
    waits.append(step)
    mine = packed[pl.ds(pl.multiple_of(core * n2, n2), n2), :].astype(F32)
    for_x[...] = (mine + from_core[...].astype(F32)).astype(BF16)

    steps = []
    for k in range(1, 4):
        there = pl.multiple_of(lax.rem(x + k, 4) * n8, n8)
        steps.append(copy(for_x.at[pl.ds(there, n8)], from_x.at[k - 1], x_sem, k - 1, at_x(k)))
        steps[-1].start()
    tot = for_x[pl.ds(pl.multiple_of(x * n8, n8), n8), :].astype(F32)
    for k in range(1, 4):
        steps[k - 1].wait_recv()
        tot += from_x[k - 1].astype(F32)
    for_y[...] = tot.astype(BF16)
    waits += steps

    steps = []
    for k in range(1, 8):
        there = pl.multiple_of(lax.rem(y + k, 8) * n64, 16)
        steps.append(copy(for_y.at[pl.ds(there, n64)], from_y.at[k - 1], y_sem, k - 1, at_y(k)))
        steps[-1].start()
    tot = for_y[pl.ds(pl.multiple_of(y * n64, 16), n64), :].astype(F32)
    for k in range(1, 8):
        steps[k - 1].wait_recv()
        tot += from_y[k - 1].astype(F32)
    for j in range(16):
        for_z[j] = tot[j * n1024 : (j + 1) * n1024]
    waits += steps

    steps = []
    for k in range(1, 16):
        there = lax.rem(z + k, 16)
        steps.append(copy(for_z.at[there], from_z.at[k - 1], z_sem, k - 1, at_z(k)))
        steps[-1].start()
    tot = for_z[z]
    for k in range(1, 16):
        steps[k - 1].wait_recv()
        tot += from_z[k - 1]
    waits += steps
    final[z] = tot * inverse
    steps = []
    for k in range(1, 16):
        steps.append(copy(final.at[z], final.at[z], zg_sem, k - 1, at_z(k)))
        steps[-1].start()
    for k in range(1, 16):
        steps[k - 1].wait_recv()
    waits += steps

    whole = jnp.concatenate([final[j] for j in range(16)], axis=0).astype(BF16)
    home = pl.ds(pl.multiple_of(((core * 4 + x) * 8 + y) * n64, 16), n64)
    gathered[home, :] = whole
    steps = []
    for k in range(1, 8):
        steps.append(copy(gathered.at[home], gathered.at[home], yg_sem, k - 1, at_y(k)))
        steps[-1].start()
    for k in range(1, 8):
        steps[k - 1].wait_recv()
    waits += steps
    home = pl.ds(pl.multiple_of((core * 4 + x) * n8, n8), n8)
    steps = []
    for k in range(1, 4):
        steps.append(copy(gathered.at[home], gathered.at[home], xg_sem, k - 1, at_x(k)))
        steps[-1].start()
    for k in range(1, 4):
        steps[k - 1].wait_recv()
    waits += steps
    home = pl.ds(pl.multiple_of(core * n2, n2), n2)
    step = copy(gathered.at[home], gathered.at[home], cg_sem, 0, at_core())
    step.start()
    step.wait_recv()
    waits.append(step)

    for p, (i, j) in enumerate(pairs):
        for h in range(2):
            tile = gathered[pl.ds((2 * p + h) * BLOCK, BLOCK), :]
            projected_ref[i * BLOCK : (i + 1) * BLOCK, j * BLOCK + h * 128 : j * BLOCK + (h + 1) * 128] = tile
            if j > i:
                turned = jnp.transpose(tile.astype(F32)).astype(BF16)
                projected_ref[
                    j * BLOCK + h * 128 : j * BLOCK + (h + 1) * 128, i * BLOCK : (i + 1) * BLOCK
                ] = turned
    for j in range(count):
        cut = slice(j * BLOCK, (j + 1) * BLOCK)
        out = right[:, cut].astype(F32) - dot(left[...], projected_ref[:, cut])
        residual_ref[:, cut] = out[:share]
    for step in waits:
        step.wait_send()


def body(orbitals, potential, cell_hamiltonian, connectivity, face_nodes):
    owned, width = orbitals.shape
    cells, npc, _ = cell_hamiltonian.shape
    peers, domains = lax.axis_size("orb"), lax.axis_size("dom")
    share = owned // peers
    part = -(-share // 16) * 16
    end = cells * STRIDE
    upper = lax.reduce_precision(potential, 8, 7)
    rest = potential - upper
    middle = lax.reduce_precision(rest, 8, 7)
    lower = lax.reduce_precision(rest - middle, 8, 7)
    terms = jnp.stack([upper, middle, lower], axis=1).astype(BF16)
    nodes = jnp.concatenate([orbitals, terms, jnp.zeros((owned, 128 - width - 3), BF16)], axis=1)
    vmem = pl.BlockSpec(memory_space=pltpu.VMEM)
    steps = DEGREE + 1
    blocks = pl.pallas_call(
        functools.partial(filter_kernel, (cells, npc, owned, share, peers)),
        out_shape=jax.ShapeDtypeStruct((peers, part, 2 * width), BF16),
        in_specs=[vmem] * 6,
        out_specs=vmem,
        scratch_shapes=[
            pltpu.VMEM((steps, end + SIDE, width), BF16),
            pltpu.VMEM((cells, SPAN, SPAN), BF16),
            pltpu.VMEM((end + SIDE, width), F32),
            pltpu.VMEM((end, width), F32),
            pltpu.VMEM((cells, SPAN, 1), jnp.int32),
            pltpu.VMEM((cells, 1, SPAN), jnp.int32),
            pltpu.VMEM((end, 2 * width), BF16),
            pltpu.VMEM((steps, SIDE, width), BF16),
            pltpu.VMEM((steps, STRIDE, width), BF16),
            pltpu.VMEM((SIDE, SPAN), BF16),
            pltpu.SemaphoreType.DMA((steps, 2)),
            pltpu.SemaphoreType.DMA((steps, 2)),
            pltpu.SemaphoreType.DMA((2,)),
        ],
        compiler_params=pltpu.CompilerParams(
            collective_id=0, has_side_effects=True, vmem_limit_bytes=60 << 20
        ),
        name="chebyshev_filter",
    )(
        nodes,
        cell_hamiltonian,
        connectivity,
        connectivity.T,
        face_nodes[None, :],
        face_nodes[:, None],
    )
    rows = lax.all_to_all(blocks, "orb", split_axis=0, concat_axis=0, tiled=True)
    orbs = peers * width
    count = orbs // BLOCK
    size = count * (count + 1) // 2 * 2 * BLOCK
    residual, projected = pl.pallas_call(
        functools.partial(project_kernel, (share, 1.0 / (owned * domains))),
        out_shape=(
            jax.ShapeDtypeStruct((share, orbs), F32),
            jax.ShapeDtypeStruct((orbs, orbs), BF16),
        ),
        in_specs=[vmem],
        out_specs=(vmem, vmem),
        scratch_shapes=[
            pltpu.VMEM((part, orbs), BF16),
            pltpu.VMEM((part, orbs), BF16),
            pltpu.VMEM((size, 128), BF16),
            pltpu.VMEM((size // 2, 128), BF16),
            pltpu.VMEM((size // 2, 128), BF16),
            pltpu.VMEM((3, size // 8, 128), BF16),
            pltpu.VMEM((size // 8, 128), BF16),
            pltpu.VMEM((7, size // 64, 128), BF16),
            pltpu.VMEM((16, size // 1024, 128), F32),
            pltpu.VMEM((15, size // 1024, 128), F32),
            pltpu.VMEM((16, size // 1024, 128), F32),
            pltpu.VMEM((size, 128), BF16),
            pltpu.SemaphoreType.DMA((2, 1)),
            pltpu.SemaphoreType.DMA((2, 3)),
            pltpu.SemaphoreType.DMA((2, 7)),
            pltpu.SemaphoreType.DMA((2, 15)),
            pltpu.SemaphoreType.DMA((2, 15)),
            pltpu.SemaphoreType.DMA((2, 7)),
            pltpu.SemaphoreType.DMA((2, 3)),
            pltpu.SemaphoreType.DMA((2, 1)),
        ],
        compiler_params=pltpu.CompilerParams(
            collective_id=1, has_side_effects=True, vmem_limit_bytes=60 << 20
        ),
        name="project",
    )(rows)
    return residual, projected


def solution(mesh):
    return jax.shard_map(
        body,
        mesh=mesh,
        in_specs=(P("dom", "orb"), P("dom"), P("dom", None, None), P("dom", None), P("dom")),
        out_specs=(P(("dom", "orb"), None), P()),
        check_vma=False,
    )
```

time: 1090 us -> 200 us (0.18)
  blocking collectives: 430 us -> 43.9 us
  waiting for transfers between devices: 361 us -> 0 us
  Pallas kernels: 0 us -> 138 us
  other arithmetic: 138 us -> 0.76 us
  local copies, waits for them, and re-layouts: 80.6 us -> 16.1 us
  starting transfers between devices: 55.1 us -> 0 us
  between operations: 14.4 us -> 0.7 us
  matrix products: 13.4 us -> 0 us
    psum x1 -> x0, blocking collectives: 397 us -> none  [body(): share = lax.psum(share, 'dom')]
    reduce_scatter x1 -> x0, waiting for transfers between devices: 197 us -> none  [body(): lax.psum_scatter(jnp.einsum('ri,rj->ij', node_rows, image_rows, preferred...]
    all_gather x1 -> x0, waiting for transfers between devices: 150 us -> none  [body(): lax.all_gather(share.astype(jnp.bfloat16), 'orb', axis=0, tiled=True)]
    pallas_call x0 -> x2, Pallas kernels: none -> 138 us  [the longest x1 74.8 us: body(): pl.pallas_call(functools.partial(filter_kernel, (cells, npc, owned, share...]
    scatter-add x10 -> x0, other arithmetic: 107 us -> none  [the longest x5 91.8 us: apply_hamiltonian(): summed = jnp.zeros((values.shape[0], extended.shape[1]), jnp.float32).at[...]
    gather x20 -> x0, local copies, waits for them, and re-layouts: 50.9 us -> none  [the longest x15 45.6 us: apply_hamiltonian(): cell_values = jnp.take(extended, connectivity, axis=1)]
    ppermute x10 -> x0, starting transfers between devices: 35.7 us -> none  [from_behind(): return lax.ppermute(block, axis, route)]
    transpose x10 -> x0, local copies, waits for them, and re-layouts: 21.3 us -> none  [apply_hamiltonian(): jnp.einsum('kij,okj->oki', cell_hamiltonian, cell_values, preferred_eleme...]
  transfers between devices with their start and end apart: 13 -> 0, of which waited for: 6 -> 0; matrix products, arithmetic and copies ran while one was open for 5% -> 0% of each run, Pallas kernels for 0% -> 0%
where the time goes in v1:
time: 200 us; the launch traced here: 199 us
  Pallas kernels  138 us (69%)
  blocking collectives  43.9 us (22%)
  local copies, waits for them, and re-layouts  16.1 us (8%)
    pallas_call x1, Pallas kernels, body(): pl.pallas_call(functools.partial(filter_kernel, (cells, npc, owned, share...  74.8 us
    pallas_call x1, Pallas kernels, body(): pl.pallas_call(functools.partial(project_kernel, (share, 1.0 / (owned * d...  62.8 us
    all_to_all x1, blocking collectives, body(): lax.all_to_all(blocks, 'orb', split_axis=0, concat_axis=0, tiled=True)  43.9 us
    unnamed x7, local copies, waits for them, and re-layouts  10.1 us

profile of v1, /device:TPU:1, one launch (start us, length us, event | category | flops | bytes accessed | tf_op | source)
XLA Modules:
  0.0 199.1 jit_solution(5990000096885536409)
XLA Ops:
  0.6 0.0 copy-start
  0.6 0.8 fusion.1
  1.4 1.3 copy.17.face_col_ref
  2.7 1.5 copy.15
  4.3 0.4 stack.19
  4.6 0.4 stack.18
  5.0 0.4 stack.17
  5.4 0.0 copy-done
  5.4 0.3 copy.11
  5.8 3.2 %copy.16.mats_ref = bf16[8,343,343]{2,1,0:T(8,128)(2,1)} copy(bf16[8,343,343]{2,0,1:T(8,128)(2,1)} %param.7) | data formatting | bytes 3764768 | tf_op args[2]
  9.0 0.1 broadcast_in_dim.9
  9.1 3.5 %concatenate.4.nodes_ref = bf16[2352,128]{1,0:T(8,128)(2,1)} concatenate(bf16[2352,64]{1,0:T(8,128)(2,1)S(1)} %copy.11, bf16[2352,1]{1,0:T(8,128)(2,1)S(1)} %stack.17, bf16[2352,1]{1,0:T(8,128)(2,1)S(1)} %stack.18, bf16[2352,1]{1,0:T(8,128)(2,1)S(1)} %stack.19, bf16[2352,61]{1,0:T(8,128)(2,1)S(1)} %broadcast_in_dim.9), dimensions={1} | concatenate | bytes 1204224 | tf_op jit(solution)/shard_map/concatenate | solution.py:428
  12.5 74.8 %chebyshev_filter.1 = bf16[16,160,128]{2,1,0:T(8,128)(2,1)} custom-call(bf16[2352,128]{1,0:T(8,128)(2,1)} %concatenate.4.nodes_ref, bf16[8,343,343]{2,1,0:T(8,128)(2,1)} %copy.16.mats_ref, s32[8,343]{1,0:T(8,128)} %conn_ref.1, s32[343,8]{1,0:T(8,128)} %bitcast.3, s32[1,49]{1,0:T(1,128)} %bitcast.5, s32[49,1]{1,0:T(8,128)} %copy.17.face_col_ref), custom_call_target="tpu_custom_call" | custom-call | tf_op jit(solution)/shard_map/chebyshev_filter/pallas_call | solution.py:431
  87.4 43.9 %all_to_all.5.rows_ref = bf16[16,160,128]{2,1,0:T(8,128)(2,1)} all-to-all(bf16[16,160,128]{2,1,0:T(8,128)(2,1)} %chebyshev_filter.1), channel_id=1, replica_groups=mesh['dom'=64,'orb'=16] {'orb'}, dimensions={0} | all-to-all | bytes 1310720 | tf_op jit(solution)/shard_map/all_to_all | solution.py:463
  131.3 62.8 %project.1 = (f32[147,1024]{1,0:T(8,128)}, bf16[1024,1024]{1,0:T(8,128)(2,1)}) custom-call(bf16[16,160,128]{2,1,0:T(8,128)(2,1)} %all_to_all.5.rows_ref), custom_call_target="tpu_custom_call" | custom-call | tf_op jit(solution)/shard_map/project/pallas_call | solution.py:467
  194.1 2.0 copy.20
  196.0 3.1 %copy.21 = bf16[1024,1024]{1,0:T(8,128)(2,1)} copy(bf16[1024,1024]{1,0:T(8,128)(2,1)} %get-tuple-element.8) | data formatting | bytes 4194304
Async XLA Ops:
  0.6 4.8 %copy-start = (bf16[2352,64]{0,1:T(8,128)(2,1)S(1)}, bf16[2352,64]{0,1:T(8,128)(2,1)}, u32[]{:S(2)}) copy-start(bf16[2352,64]{0,1:T(8,128)(2,1)} %param.5) | copy-start | bytes 903172

commit v2 on v0

v2 whole, which is shorter than its diff:
```python
import functools

import jax
import jax.numpy as jnp
from jax import lax
from jax.experimental import pallas as pl
from jax.experimental.pallas import tpu as pltpu
from jax.sharding import PartitionSpec as P

DEGREE = 4
MESH = pl.DeviceIdType.MESH
F32 = jnp.float32
BF16 = jnp.bfloat16

filter_center = 1.5
filter_half = 2.0

SIDE = 64
STRIDE = 320
SPAN = STRIDE + SIDE


def prefix_tables(n):
    before = lax.broadcasted_iota(jnp.int32, (n, n), 0) < lax.broadcasted_iota(jnp.int32, (n, n), 1)
    after = lax.broadcasted_iota(jnp.int32, (n, n), 0) > lax.broadcasted_iota(jnp.int32, (n, n), 1)
    return before.astype(F32).astype(BF16), after.astype(F32).astype(BF16)


def dot(a, b):
    return jnp.dot(a, b, preferred_element_type=F32)


def equal(a, b):
    return (a == b).astype(F32)


BLOCK = 256


def step_kernel(
    sizes,
    nodes_ref,
    pot_ref,
    mats_ref,
    conn_ref,
    face_ref,
    left_ref,
    right_ref,
    sum_ref,
    table,
    values,
    cellmats,
    total,
    pots,
    ids_col,
    ids_row,
    both,
    ghosts,
    behind,
    behind_mat,
    filtered_out,
    filtered_in,
    image_out,
    image_in,
    packed,
    from_core,
    for_x,
    from_x,
    for_y,
    from_y,
    for_z,
    from_z,
    final,
    gathered,
    halo_sem,
    mat_sem,
    filtered_sem,
    image_sem,
    core_sem,
    x_sem,
    y_sem,
    z_sem,
    zg_sem,
    yg_sem,
    xg_sem,
    cg_sem,
):
    cells, npc, owned, share, inverse = sizes
    dom, orb = lax.axis_index("dom"), lax.axis_index("orb")
    domains = lax.axis_size("dom")
    y, z_lo = dom // 8, lax.rem(dom, 8)
    x, z_hi, core = orb // 4, lax.rem(orb // 2, 2), lax.rem(orb, 2)
    z = z_hi * 8 + z_lo
    nxt = {"dom": lax.rem(dom + 1, domains), "orb": orb}
    prv = {"dom": lax.rem(dom + domains - 1, domains), "orb": orb}

    def at_core():
        return {"dom": dom, "orb": orb + 1 - 2 * core}

    def at_x(k):
        return {"dom": dom, "orb": lax.rem(x + k, 4) * 4 + z_hi * 2 + core}

    def at_y(k):
        return {"dom": lax.rem(y + k, 8) * 8 + z_lo, "orb": orb}

    def at_z(k):
        there = lax.rem(z + k, 16)
        return {"dom": y * 8 + lax.rem(there, 8), "orb": x * 4 + (there // 8) * 2 + core}

    def orb_at(k):
        return (
            lax.rem(x + k // 4, 4) * 4 + lax.rem(z_hi + k // 2 % 2, 2) * 2 + lax.rem(core + k % 2, 2)
        )

    far_first = [k for k in range(1, 16) if k // 2 % 2] + [k for k in range(1, 16) if not k // 2 % 2]

    def copy(src, dst, sems, k, peer):
        return pltpu.make_async_remote_copy(
            src_ref=src,
            dst_ref=dst,
            send_sem=sems.at[0, k],
            recv_sem=sems.at[1, k],
            device_id=peer,
            device_id_type=MESH,
        )

    barrier = pltpu.get_barrier_semaphore()
    peers = [prv, nxt, at_core()]
    peers += [at_x(k) for k in range(1, 4)]
    peers += [at_y(k) for k in range(1, 8)]
    peers += [at_z(k) for k in range(1, 16)]
    peers += [{"dom": dom, "orb": orb_at(k)} for k in range(1, 16)]
    for peer in peers:
        pl.semaphore_signal(barrier, inc=1, device_id=peer, device_id_type=MESH)

    width = values.shape[2]
    pot = pot_ref[...]
    upper = pot.astype(BF16)
    rest = pot - upper.astype(F32)
    middle = rest.astype(BF16)
    lower = (rest - middle.astype(F32)).astype(BF16)
    table[pl.ds(0, width), :] = nodes_ref[...]
    place = lax.broadcasted_iota(jnp.int32, (16, owned), 0)
    terms = jnp.where(
        place == 0,
        upper.astype(F32),
        jnp.where(place == 1, middle.astype(F32), jnp.where(place == 2, lower.astype(F32), 0.0)),
    )
    table[pl.ds(width, 16), :] = terms.astype(BF16)

    conn = conn_ref[...].astype(F32)
    turned = jnp.transpose(conn)
    rows = [conn[c : c + 1, :] for c in range(cells)]
    cols = [turned[:, c : c + 1] for c in range(cells)]
    face_row = face_ref[...].astype(F32)
    face_col = jnp.transpose(jnp.broadcast_to(face_row, (8, face_row.shape[1])))[:, :1]
    faces = face_row.shape[1]

    low = [equal(cols[c], rows[c + 1]) for c in range(cells - 1)]
    high = [equal(cols[c + 1], rows[c]) for c in range(cells - 1)]
    first_row = equal(face_col, rows[0])
    first_col = equal(cols[0], face_row)
    bottom_row = [jnp.sum(first_row, axis=0, keepdims=True)]
    bottom_row += [jnp.sum(low[c], axis=0, keepdims=True) for c in range(cells - 1)]
    bottom_col = [jnp.sum(first_col, axis=1, keepdims=True)]
    bottom_col += [jnp.sum(high[c], axis=1, keepdims=True) for c in range(cells - 1)]
    top_row = [jnp.sum(high[c], axis=0, keepdims=True) for c in range(cells - 1)]
    top_row += [(rows[-1] >= owned).astype(F32)]
    top_col = [jnp.sum(low[c], axis=1, keepdims=True) for c in range(cells - 1)]
    top_col += [(cols[-1] >= owned).astype(F32)]

    before, after = prefix_tables(npc)
    inner_row = [1.0 - bottom_row[c] - top_row[c] for c in range(cells)]
    inner_col = [1.0 - bottom_col[c] - top_col[c] for c in range(cells)]
    stacked_row = jnp.concatenate(bottom_row + inner_row, axis=0).astype(BF16)
    stacked_col = jnp.concatenate(bottom_col + inner_col, axis=1).astype(BF16)
    rank_row = dot(stacked_row, before)
    rank_col = dot(after, stacked_col)
    place_row = lax.broadcasted_iota(jnp.int32, (faces, 1), 0).astype(F32)
    place_col = lax.broadcasted_iota(jnp.int32, (1, faces), 1).astype(F32)
    low_row = [jnp.sum(first_row * place_row, axis=0, keepdims=True)]
    low_row += [rank_row[c : c + 1] for c in range(1, cells)]
    low_col = [jnp.sum(first_col * place_col, axis=1, keepdims=True)]
    low_col += [rank_col[:, c : c + 1] for c in range(1, cells)]
    high_row = [jnp.sum(high[c] * low_col[c + 1], axis=0, keepdims=True) for c in range(cells - 1)]
    high_row += [rows[-1] - owned]
    high_col = [jnp.sum(low[c] * low_row[c + 1], axis=1, keepdims=True) for c in range(cells - 1)]
    high_col += [cols[-1] - owned]

    def slots(bottom, top, low_rank, high_rank, inner_rank):
        inner = SIDE + inner_rank
        return jnp.where(bottom > 0.5, low_rank, jnp.where(top > 0.5, STRIDE + high_rank, inner)).astype(
            jnp.int32
        )

    def spread_of(c):
        slot_row = slots(
            bottom_row[c], top_row[c], low_row[c], high_row[c], rank_row[cells + c : cells + c + 1]
        )
        slot_col = slots(
            bottom_col[c], top_col[c], low_col[c], high_col[c], rank_col[:, cells + c : cells + c + 1]
        )
        down = equal(lax.broadcasted_iota(jnp.int32, (SPAN, npc), 0), slot_row)
        across = equal(slot_col, lax.broadcasted_iota(jnp.int32, (npc, SPAN), 1))
        return down, across

    order = [cells - 1] + list(range(cells - 1))
    for c in order:
        down, across = spread_of(c)
        named = rows[c] + 1.0
        ids_col[c] = (jnp.sum(down * named, axis=1, keepdims=True) - 1.0).astype(jnp.int32)
        named = cols[c] + 1.0
        ids_row[c] = (jnp.sum(across * named, axis=0, keepdims=True) - 1.0).astype(jnp.int32)
        half = dot(down.astype(BF16), mats_ref[c]).astype(BF16)
        cellmats[c] = dot(half, across.astype(BF16)).astype(BF16)

    pl.semaphore_wait(barrier, len(peers))
    waits = []
    mat_copy = copy(cellmats.at[cells - 1, pl.ds(STRIDE, SIDE)], behind_mat, mat_sem, 0, nxt)
    mat_copy.start()
    waits.append(mat_copy)

    def take(c, carry):
        pick = equal(
            ids_col[c, pl.ds(0, STRIDE), :], lax.broadcasted_iota(jnp.int32, (STRIDE, owned), 1)
        )
        found = lax.dot_general(
            pick.astype(BF16), table[...], (((1,), (1,)), ((), ())), preferred_element_type=F32
        )
        start = pl.multiple_of(c * STRIDE, STRIDE)
        values[0, pl.ds(start, STRIDE), :] = found[:, :width].astype(BF16)
        pot = found[:, width : width + 1] + found[:, width + 1 : width + 2] + found[:, width + 2 : width + 3]
        pots[pl.ds(start, STRIDE), :] = jnp.broadcast_to(pot, (STRIDE, width))
        return carry

    lax.fori_loop(0, cells, take, 0)

    part = filtered_out.shape[1]
    padded = left_ref.shape[0] // 2

    def give(out):
        def one(b, carry):
            row = lax.broadcasted_iota(jnp.int32, (2 * padded, STRIDE), 0)
            low = jnp.where(row < part, row, -2 - owned)
            high = jnp.where(row < padded + share - part, row - padded + part, -2 - owned)
            target = jnp.where(row < padded, low, high) + b * share
            found = jnp.zeros((2 * padded, 2 * width), F32)
            for c in range(cells):
                pick = equal(ids_row[c, :, pl.ds(0, STRIDE)], target)
                found += dot(pick.astype(BF16), both[pl.ds(c * STRIDE, STRIDE), :])
            lane = lax.broadcasted_iota(jnp.int32, (padded, 2 * width), 1)
            out[b] = jnp.where(lane < width, found[:padded], found[padded:])[:part].astype(BF16)
            return carry

        lax.fori_loop(0, 16, one, 0)

    def exchange(out, into, sems):
        steps = {}
        for k in far_first:
            there = orb_at(k)
            steps[k] = copy(out.at[there], into.at[orb], sems, k - 1, {"dom": dom, "orb": there})
            steps[k].start()
        into[orb] = out[orb]
        return [steps[k] for k in range(1, 16)]

    end = cells * STRIDE
    has_next = (dom < domains - 1).astype(F32)
    has_prev = (dom > 0).astype(F32)
    for step in range(DEGREE + 1):
        back = copy(values.at[step, pl.ds(0, SIDE)], ghosts.at[step], halo_sem, 2 * step, prv)
        ahead = copy(
            values.at[step, pl.ds(end - STRIDE, STRIDE)], behind.at[step], halo_sem, 2 * step + 1, nxt
        )
        back.start()
        ahead.start()
        waits += [back, ahead]
        own = pl.ds(0, end)
        if step == DEGREE:
            both[:, :width] = values[step, own, :]
            both[:, width:] = values[step, own, :]
            give(filtered_out)
            filtered_steps = exchange(filtered_out, filtered_in, filtered_sem)
        total[...] = jnp.zeros_like(total)
        for c in range(cells - 1):
            span = pl.ds(c * STRIDE, SPAN)
            total[span, :] += dot(cellmats[c], values[step, span, :])
        back.wait_recv()
        values[step, pl.ds(end, SIDE), :] = (ghosts[step].astype(F32) * has_next).astype(BF16)
        span = pl.ds(end - STRIDE, SPAN)
        total[span, :] += dot(cellmats[cells - 1], values[step, span, :])
        if step == 0:
            mat_copy.wait_recv()
        ahead.wait_recv()
        shared = dot(behind_mat[:, :STRIDE], behind[step]) + dot(
            behind_mat[:, STRIDE:], values[step, pl.ds(0, SIDE), :]
        )
        total[pl.ds(0, SIDE), :] += shared * has_prev
        current = values[step, own, :].astype(F32)
        image = total[own, :] + pots[...] * current
        if step == 0:
            values[1, own, :] = ((image - filter_center * current) / filter_half).astype(BF16)
        elif step < DEGREE:
            previous = values[step - 1, own, :].astype(F32)
            scaled = 2.0 * (image - filter_center * current) / filter_half
            values[step + 1, own, :] = (scaled - previous).astype(BF16)
        else:
            both[:, :width] = image.astype(BF16)
            both[:, width:] = image.astype(BF16)
    give(image_out)
    image_steps = exchange(image_out, image_in, image_sem)
    waits += filtered_steps + image_steps

    lanes = 2 * width
    lane = lax.broadcasted_iota(jnp.int32, (part, lanes), 1)

    def assemble(into, out):
        out[...] = jnp.zeros_like(out)
        for m in range(8):
            a, b = into[2 * m].astype(F32), into[2 * m + 1].astype(F32)
            cut = pl.ds(m * lanes, lanes)
            low = jnp.where(lane < width, a, pltpu.roll(b, width, 1))
            high = jnp.where(lane < width, pltpu.roll(a, width, 1), b)
            out[pl.ds(0, part), cut] = low.astype(BF16)
            out[pl.ds(padded, part), cut] = high.astype(BF16)

    for step in filtered_steps:
        step.wait_recv()
    assemble(filtered_in, left_ref)
    for step in image_steps:
        step.wait_recv()
    assemble(image_in, right_ref)

    count = left_ref.shape[1] // BLOCK
    pairs = [(i, j) for i in range(count) for j in range(i, count)]
    for p, (i, j) in enumerate(pairs):
        block = lax.dot_general(
            left_ref[:, i * BLOCK : (i + 1) * BLOCK],
            right_ref[:, j * BLOCK : (j + 1) * BLOCK],
            (((0,), (0,)), ((), ())),
            preferred_element_type=F32,
        ).astype(BF16)
        packed[pl.ds((2 * p) * BLOCK, BLOCK), :] = block[:, :128]
        packed[pl.ds((2 * p + 1) * BLOCK, BLOCK), :] = block[:, 128:]
    size = packed.shape[0]
    n2, n8, n64, n1024 = size // 2, size // 8, size // 64, size // 1024

    def at(piece, rows):
        return pl.ds(pl.multiple_of(piece * rows, 16), rows)

    order = (1, 3, 2, 0)
    steps = {}
    for k in order:
        piece = (1 - core) * 4 + lax.rem(x + k, 4)
        steps[k] = copy(packed.at[at(piece, n8)], from_core.at[k], core_sem, k, at_core())
        steps[k].start()
    waits += [steps[k] for k in order]
    x_steps = {}
    for k in order:
        steps[k].wait_recv()
        mine = packed[at(core * 4 + lax.rem(x + k, 4), n8), :].astype(F32) + from_core[k].astype(F32)
        if k:
            for_x[k] = mine.astype(BF16)
            x_steps[k] = copy(for_x.at[k], from_x.at[k - 1], x_sem, k - 1, at_x(k))
            x_steps[k].start()
    waits += [x_steps[k] for k in range(1, 4)]
    tot = mine
    for k in range(1, 4):
        x_steps[k].wait_recv()
        tot += from_x[k - 1].astype(F32)
    for_y[...] = tot.astype(BF16)

    steps = {}
    for k in (4, 3, 5, 2, 6, 1, 7):
        steps[k] = copy(for_y.at[at(lax.rem(y + k, 8), n64)], from_y.at[k - 1], y_sem, k - 1, at_y(k))
        steps[k].start()
    tot = for_y[at(y, n64), :].astype(F32)
    for k in (1, 7, 2, 6, 3, 5, 4):
        steps[k].wait_recv()
        tot += from_y[k - 1].astype(F32)
        waits.append(steps[k])
    for j in range(16):
        for_z[j] = tot[j * n1024 : (j + 1) * n1024]

    steps = {}
    spread = [8, 7, 9, 6, 10, 5, 11, 4, 12, 3, 13, 2, 14, 1, 15]
    for k in spread:
        there = lax.rem(z + k, 16)
        steps[k] = copy(for_z.at[there], from_z.at[k - 1], z_sem, k - 1, at_z(k))
        steps[k].start()
    tot = for_z[z]
    for k in reversed(spread):
        steps[k].wait_recv()
        tot += from_z[k - 1]
        waits.append(steps[k])
    final[z] = tot * inverse
    steps = {}
    for k in spread:
        steps[k] = copy(final.at[z], final.at[z], zg_sem, k - 1, at_z(k))
        steps[k].start()
    for k in reversed(spread):
        steps[k].wait_recv()
        waits.append(steps[k])

    whole = jnp.concatenate([final[j] for j in range(16)], axis=0).astype(BF16)
    group = core * 4 + x
    home = at(group * 8 + y, n64)
    gathered[home, :] = whole
    y_steps = {}
    for k in (4, 3, 5, 2, 6, 1, 7):
        y_steps[k] = copy(gathered.at[home], gathered.at[home], yg_sem, k - 1, at_y(k))
        y_steps[k].start()
    x_steps = {}
    for r in (0, 1, 7, 2, 6, 3, 5, 4):
        if r:
            y_steps[r].wait_recv()
            waits.append(y_steps[r])
        spot = at(group * 8 + lax.rem(y + 8 - r, 8), n64)
        for k in (2, 1, 3):
            x_steps[k, r] = copy(gathered.at[spot], gathered.at[spot], xg_sem, (k - 1) * 8 + r, at_x(k))
            x_steps[k, r].start()
    core_steps = {}
    for k in (0, 1, 3, 2):
        if k:
            for r in (0, 1, 7, 2, 6, 3, 5, 4):
                x_steps[k, r].wait_recv()
                waits.append(x_steps[k, r])
        spot = at(core * 4 + lax.rem(x + 4 - k, 4), n8)
        core_steps[k] = copy(gathered.at[spot], gathered.at[spot], cg_sem, k, at_core())
        core_steps[k].start()
    for k in (0, 1, 3, 2):
        core_steps[k].wait_recv()
        waits.append(core_steps[k])
    sum_ref[...] = gathered[...]
    for step in waits:
        step.wait_send()


def residual_kernel(left_ref, right_ref, sum_ref, residual_ref, projected_ref):
    share = residual_ref.shape[0]
    padded = left_ref.shape[0] // 2
    part = (share + 1) // 2
    count = left_ref.shape[1] // BLOCK
    pairs = [(i, j) for i in range(count) for j in range(i, count)]
    for p, (i, j) in enumerate(pairs):
        for h in range(2):
            tile = sum_ref[pl.ds((2 * p + h) * BLOCK, BLOCK), :]
            start = j * BLOCK + h * 128
            projected_ref[i * BLOCK : (i + 1) * BLOCK, start : start + 128] = tile
            if j > i:
                turned = jnp.transpose(tile.astype(F32)).astype(BF16)
                projected_ref[start : start + 128, i * BLOCK : (i + 1) * BLOCK] = turned
    for j in range(count):
        cut = slice(j * BLOCK, (j + 1) * BLOCK)
        out = right_ref[:, cut].astype(F32) - dot(left_ref[...], projected_ref[:, cut])
        residual_ref[:part, cut] = out[:part]
        residual_ref[part:, cut] = out[padded : padded + share - part]


def body(orbitals, potential, cell_hamiltonian, connectivity, face_nodes):
    owned, width = orbitals.shape
    cells, npc, _ = cell_hamiltonian.shape
    peers, domains = lax.axis_size("orb"), lax.axis_size("dom")
    share = owned // peers
    part = (share + 1) // 2
    padded = -(-part // 16) * 16
    end = cells * STRIDE
    orbs = peers * width
    count = orbs // BLOCK
    size = count * (count + 1) // 2 * 2 * BLOCK
    vmem = pl.BlockSpec(memory_space=pltpu.VMEM)
    steps = DEGREE + 1
    sem = pltpu.SemaphoreType.DMA
    left, right, sums = pl.pallas_call(
        functools.partial(step_kernel, (cells, npc, owned, share, 1.0 / (owned * domains))),
        out_shape=(
            jax.ShapeDtypeStruct((2 * padded, orbs), BF16),
            jax.ShapeDtypeStruct((2 * padded, orbs), BF16),
            jax.ShapeDtypeStruct((size, 128), BF16),
        ),
        in_specs=[vmem] * 5,
        out_specs=(vmem,) * 3,
        scratch_shapes=[
            pltpu.VMEM((width + 16, owned), BF16),
            pltpu.VMEM((steps, end + SIDE, width), BF16),
            pltpu.VMEM((cells, SPAN, SPAN), BF16),
            pltpu.VMEM((end + SIDE, width), F32),
            pltpu.VMEM((end, width), F32),
            pltpu.VMEM((cells, SPAN, 1), jnp.int32),
            pltpu.VMEM((cells, 1, SPAN), jnp.int32),
            pltpu.VMEM((end, 2 * width), BF16),
            pltpu.VMEM((steps, SIDE, width), BF16),
            pltpu.VMEM((steps, STRIDE, width), BF16),
            pltpu.VMEM((SIDE, SPAN), BF16),
            pltpu.VMEM((peers, part, 2 * width), BF16),
            pltpu.VMEM((peers, part, 2 * width), BF16),
            pltpu.VMEM((peers, part, 2 * width), BF16),
            pltpu.VMEM((peers, part, 2 * width), BF16),
            pltpu.VMEM((size, 128), BF16),
            pltpu.VMEM((4, size // 8, 128), BF16),
            pltpu.VMEM((4, size // 8, 128), BF16),
            pltpu.VMEM((3, size // 8, 128), BF16),
            pltpu.VMEM((size // 8, 128), BF16),
            pltpu.VMEM((7, size // 64, 128), BF16),
            pltpu.VMEM((16, size // 1024, 128), F32),
            pltpu.VMEM((15, size // 1024, 128), F32),
            pltpu.VMEM((16, size // 1024, 128), F32),
            pltpu.VMEM((size, 128), BF16),
            sem((2, 2 * steps)),
            sem((2, 1)),
            sem((2, 15)),
            sem((2, 15)),
            sem((2, 4)),
            sem((2, 3)),
            sem((2, 7)),
            sem((2, 15)),
            sem((2, 15)),
            sem((2, 7)),
            sem((2, 24)),
            sem((2, 4)),
        ],
        compiler_params=pltpu.CompilerParams(
            collective_id=0, has_side_effects=True, vmem_limit_bytes=60 << 20
        ),
        name="filter_and_project",
    )(orbitals.T, potential[None, :], cell_hamiltonian, connectivity, face_nodes[None, :])
    return pl.pallas_call(
        residual_kernel,
        out_shape=(
            jax.ShapeDtypeStruct((share, orbs), F32),
            jax.ShapeDtypeStruct((orbs, orbs), BF16),
        ),
        in_specs=[vmem] * 3,
        out_specs=(vmem, vmem),
        compiler_params=pltpu.CompilerParams(vmem_limit_bytes=60 << 20),
        name="residual",
    )(left, right, sums)


def solution(mesh):
    return jax.shard_map(
        body,
        mesh=mesh,
        in_specs=(P("dom", "orb"), P("dom"), P("dom", None, None), P("dom", None), P("dom")),
        out_specs=(P(("dom", "orb"), None), P()),
        check_vma=False,
    )
```

time: 1090 us -> 166 us (0.15)
  blocking collectives: 430 us -> 0 us
  waiting for transfers between devices: 361 us -> 0 us
  Pallas kernels: 0 us -> 160 us
  other arithmetic: 138 us -> 0 us
  local copies, waits for them, and re-layouts: 80.6 us -> 4.52 us
  starting transfers between devices: 55.1 us -> 0 us
  between operations: 14.4 us -> 0.64 us
  matrix products: 13.4 us -> 0 us
    psum x1 -> x0, blocking collectives: 397 us -> none  [body(): share = lax.psum(share, 'dom')]
    reduce_scatter x1 -> x0, waiting for transfers between devices: 197 us -> none  [body(): lax.psum_scatter(jnp.einsum('ri,rj->ij', node_rows, image_rows, preferred...]
    pallas_call x0 -> x2, Pallas kernels: none -> 160 us  [the longest x1 157 us: body(): pl.pallas_call(functools.partial(step_kernel, (cells, npc, owned, share,...]
    all_gather x1 -> x0, waiting for transfers between devices: 150 us -> none  [body(): lax.all_gather(share.astype(jnp.bfloat16), 'orb', axis=0, tiled=True)]
    scatter-add x10 -> x0, other arithmetic: 107 us -> none  [the longest x5 91.8 us: apply_hamiltonian(): summed = jnp.zeros((values.shape[0], extended.shape[1]), jnp.float32).at[...]
    gather x20 -> x0, local copies, waits for them, and re-layouts: 50.9 us -> none  [the longest x15 45.6 us: apply_hamiltonian(): cell_values = jnp.take(extended, connectivity, axis=1)]
    ppermute x10 -> x0, starting transfers between devices: 35.7 us -> none  [from_behind(): return lax.ppermute(block, axis, route)]
    all_to_all x1 -> x0, blocking collectives: 33 us -> none  [body(): lax.all_to_all(image.T, 'orb', split_axis=0, concat_axis=1, tiled=True)]
  transfers between devices with their start and end apart: 13 -> 0, of which waited for: 6 -> 0; matrix products, arithmetic and copies ran while one was open for 5% -> 0% of each run, Pallas kernels for 0% -> 0%
where the time goes in v2:
time: 166 us; the launch traced here: 165 us
  Pallas kernels  160 us (96%)
  local copies, waits for them, and re-layouts  4.52 us (3%)
    pallas_call x1, Pallas kernels, body(): pl.pallas_call(functools.partial(step_kernel, (cells, npc, owned, share,...  157 us
    pallas_call x1, Pallas kernels, body(): pl.pallas_call(residual_kernel, out_shape=(jax.ShapeDtypeStruct((share, o...  3.6 us

profile of v2, /device:TPU:1, one launch (start us, length us, event | category | flops | bytes accessed | tf_op | source)
XLA Modules:
  0.0 165.5 jit_solution(11318164029540730852)
XLA Ops:
  0.6 1.3 broadcast_in_dim.6.pot_ref
  1.9 3.2 %copy.7.mats_ref = bf16[8,343,343]{2,1,0:T(8,128)(2,1)} copy(bf16[8,343,343]{2,0,1:T(8,128)(2,1)} %param.7) | data formatting | bytes 3764768 | tf_op args[2]
  5.2 156.7 %filter_and_project.1 = (bf16[160,1024]{1,0:T(8,128)(2,1)}, bf16[160,1024]{1,0:T(8,128)(2,1)}, bf16[5120,128]{1,0:T(8,128)(2,1)}) custom-call(bf16[64,2352]{1,0:T(8,128)(2,1)} %bitcast.2, f32[1,2352]{1,0:T(1,128)} %broadcast_in_dim.6.pot_ref, bf16[8,343,343]{2,1,0:T(8,128)(2,1)} %copy.7.mats_ref, s32[8,343]{1,0:T(8,128)} %conn_ref.1, s32[1,49]{1,0:T(1,128)} %bitcast.3), custom_call_target="tpu_custom_call" | custom-call | tf_op jit(solution)/shard_map/filter_and_project/pallas_call | solution.py:473
  161.9 3.6 %residual.1 = (f32[147,1024]{1,0:T(8,128)}, bf16[1024,1024]{1,0:T(8,128)(2,1)}) custom-call(bf16[160,1024]{1,0:T(8,128)(2,1)} %get-tuple-element.5.left_ref, bf16[160,1024]{1,0:T(8,128)(2,1)} %get-tuple-element.6.right_ref, bf16[5120,128]{1,0:T(8,128)(2,1)} %get-tuple-element.7.sum_ref), custom_call_target="tpu_custom_call" | custom-call | tf_op jit(solution)/shard_map/residual/pallas_call | solution.py:526

commit v3 on v2

--- a/solution.py
+++ b/solution.py
@@ -107,12 +107,13 @@
         there = lax.rem(z + k, 16)
         return {"dom": y * 8 + lax.rem(there, 8), "orb": x * 4 + (there // 8) * 2 + core}
 
-    def orb_at(k):
+    def orb_at(v):
+        u = lax.rem(v, 8)
         return (
-            lax.rem(x + k // 4, 4) * 4 + lax.rem(z_hi + k // 2 % 2, 2) * 2 + lax.rem(core + k % 2, 2)
-        )
-
-    far_first = [k for k in range(1, 16) if k // 2 % 2] + [k for k in range(1, 16) if not k // 2 % 2]
+            lax.rem(x + u // 2, 4) * 4 + lax.rem(z_hi + 1 - v // 8, 2) * 2 + lax.rem(core + lax.rem(u, 2), 2)
+        )
+
+    others = [v for v in range(16) if v != 8]
 
     def copy(src, dst, sems, k, peer):
         return pltpu.make_async_remote_copy(
@@ -129,7 +130,7 @@
     peers += [at_x(k) for k in range(1, 4)]
     peers += [at_y(k) for k in range(1, 8)]
     peers += [at_z(k) for k in range(1, 16)]
-    peers += [{"dom": dom, "orb": orb_at(k)} for k in range(1, 16)]
+    peers += [{"dom": dom, "orb": orb_at(v)} for v in others]
     for peer in peers:
         pl.semaphore_signal(barrier, inc=1, device_id=peer, device_id_type=MESH)
 
@@ -204,8 +205,7 @@
         across = equal(slot_col, lax.broadcasted_iota(jnp.int32, (npc, SPAN), 1))
         return down, across
 
-    order = [cells - 1] + list(range(cells - 1))
-    for c in order:
+    def place_cell(c):
         down, across = spread_of(c)
         named = rows[c] + 1.0
         ids_col[c] = (jnp.sum(down * named, axis=1, keepdims=True) - 1.0).astype(jnp.int32)
@@ -214,12 +214,6 @@
         half = dot(down.astype(BF16), mats_ref[c]).astype(BF16)
         cellmats[c] = dot(half, across.astype(BF16)).astype(BF16)
 
-    pl.semaphore_wait(barrier, len(peers))
-    waits = []
-    mat_copy = copy(cellmats.at[cells - 1, pl.ds(STRIDE, SIDE)], behind_mat, mat_sem, 0, nxt)
-    mat_copy.start()
-    waits.append(mat_copy)
-
     def take(c, carry):
         pick = equal(
             ids_col[c, pl.ds(0, STRIDE), :], lax.broadcasted_iota(jnp.int32, (STRIDE, owned), 1)
@@ -233,57 +227,96 @@
         pots[pl.ds(start, STRIDE), :] = jnp.broadcast_to(pot, (STRIDE, width))
         return carry
 
-    lax.fori_loop(0, cells, take, 0)
-
-    part = filtered_out.shape[1]
-    padded = left_ref.shape[0] // 2
-
-    def give(out):
-        def one(b, carry):
-            row = lax.broadcasted_iota(jnp.int32, (2 * padded, STRIDE), 0)
-            low = jnp.where(row < part, row, -2 - owned)
-            high = jnp.where(row < padded + share - part, row - padded + part, -2 - owned)
-            target = jnp.where(row < padded, low, high) + b * share
-            found = jnp.zeros((2 * padded, 2 * width), F32)
-            for c in range(cells):
-                pick = equal(ids_row[c, :, pl.ds(0, STRIDE)], target)
-                found += dot(pick.astype(BF16), both[pl.ds(c * STRIDE, STRIDE), :])
-            lane = lax.broadcasted_iota(jnp.int32, (padded, 2 * width), 1)
-            out[b] = jnp.where(lane < width, found[:padded], found[padded:])[:part].astype(BF16)
-            return carry
-
-        lax.fori_loop(0, 16, one, 0)
-
-    def exchange(out, into, sems):
-        steps = {}
-        for k in far_first:
-            there = orb_at(k)
-            steps[k] = copy(out.at[there], into.at[orb], sems, k - 1, {"dom": dom, "orb": there})
-            steps[k].start()
-        into[orb] = out[orb]
-        return [steps[k] for k in range(1, 16)]
-
     end = cells * STRIDE
-    has_next = (dom < domains - 1).astype(F32)
-    has_prev = (dom > 0).astype(F32)
-    for step in range(DEGREE + 1):
+    waits = []
+
+    def send(step):
         back = copy(values.at[step, pl.ds(0, SIDE)], ghosts.at[step], halo_sem, 2 * step, prv)
         ahead = copy(
             values.at[step, pl.ds(end - STRIDE, STRIDE)], behind.at[step], halo_sem, 2 * step + 1, nxt
         )
         back.start()
         ahead.start()
-        waits += [back, ahead]
-        own = pl.ds(0, end)
+        waits.extend([back, ahead])
+        return back, ahead
+
+    for c in (cells - 1, 0):
+        place_cell(c)
+        lax.fori_loop(c, c + 1, take, 0)
+    pl.semaphore_wait(barrier, len(peers))
+    back, ahead = send(0)
+    mat_copy = copy(cellmats.at[cells - 1, pl.ds(STRIDE, SIDE)], behind_mat, mat_sem, 0, nxt)
+    mat_copy.start()
+    waits.append(mat_copy)
+    for c in range(1, cells - 1):
+        place_cell(c)
+    lax.fori_loop(1, cells - 1, take, 0)
+
+    part = filtered_out.shape[1]
+    padded = left_ref.shape[0] // 2
+
+    def block_of(b):
+        row = lax.broadcasted_iota(jnp.int32, (2 * padded, STRIDE), 0)
+        low = jnp.where(row < part, row, -2 - owned)
+        high = jnp.where(row < padded + share - part, row - padded + part, -2 - owned)
+        target = jnp.where(row < padded, low, high) + b * share
+        found = jnp.zeros((2 * padded, 2 * width), F32)
+        for c in range(cells):
+            pick = equal(ids_row[c, :, pl.ds(0, STRIDE)], target)
+            found += dot(pick.astype(BF16), both[pl.ds(c * STRIDE, STRIDE), :])
+        lane = lax.broadcasted_iota(jnp.int32, (padded, 2 * width), 1)
+        return jnp.where(lane < width, found[:padded], found[padded:])[:part].astype(BF16)
+
+    def exchange(out, into, sems):
+        def one_of(v):
+            there = orb_at(v)
+            return copy(out.at[there], into.at[orb], sems, v, {"dom": dom, "orb": there})
+
+        def one(v, carry):
+            there = orb_at(v)
+            out[there] = block_of(there)
+
+            @pl.when(v != 0)
+            def _():
+                one_of(v - 1 - (v == 9).astype(jnp.int32)).start()
+
+            return carry
+
+        lax.fori_loop(0, 8, one, 0)
+        lax.fori_loop(9, 16, one, 0)
+        into[orb] = block_of(orb)
+        one_of(15).start()
+        return [one_of(v) for v in others]
+
+    has_next = (dom < domains - 1).astype(F32)
+    has_prev = (dom > 0).astype(F32)
+    edges = [pl.ds(0, SIDE), pl.ds(end - STRIDE, STRIDE)]
+    middle_rows = pl.ds(SIDE, end - STRIDE - SIDE)
+
+    def update(step, some):
+        current = values[step, some, :].astype(F32)
+        image = total[some, :] + pots[some, :] * current
+        if step == 0:
+            values[1, some, :] = ((image - filter_center * current) / filter_half).astype(BF16)
+        elif step < DEGREE:
+            previous = values[step - 1, some, :].astype(F32)
+            scaled = 2.0 * (image - filter_center * current) / filter_half
+            values[step + 1, some, :] = (scaled - previous).astype(BF16)
+        else:
+            both[some, :width] = image.astype(BF16)
+            both[some, width:] = image.astype(BF16)
+
+    for step in range(DEGREE + 1):
         if step == DEGREE:
+            own = pl.ds(0, end)
             both[:, :width] = values[step, own, :]
             both[:, width:] = values[step, own, :]
-            give(filtered_out)
             filtered_steps = exchange(filtered_out, filtered_in, filtered_sem)
         total[...] = jnp.zeros_like(total)
         for c in range(cells - 1):
             span = pl.ds(c * STRIDE, SPAN)
             total[span, :] += dot(cellmats[c], values[step, span, :])
+        update(step, middle_rows)
         back.wait_recv()
         values[step, pl.ds(end, SIDE), :] = (ghosts[step].astype(F32) * has_next).astype(BF16)
         span = pl.ds(end - STRIDE, SPAN)
@@ -295,18 +328,10 @@
             behind_mat[:, STRIDE:], values[step, pl.ds(0, SIDE), :]
         )
         total[pl.ds(0, SIDE), :] += shared * has_prev
-        current = values[step, own, :].astype(F32)
-        image = total[own, :] + pots[...] * current
-        if step == 0:
-            values[1, own, :] = ((image - filter_center * current) / filter_half).astype(BF16)
-        elif step < DEGREE:
-            previous = values[step - 1, own, :].astype(F32)
-            scaled = 2.0 * (image - filter_center * current) / filter_half
-            values[step + 1, own, :] = (scaled - previous).astype(BF16)
-        else:
-            both[:, :width] = image.astype(BF16)
-            both[:, width:] = image.astype(BF16)
-    give(image_out)
+        for some in edges:
+            update(step, some)
+        if step < DEGREE:
+            back, ahead = send(step + 1)
     image_steps = exchange(image_out, image_in, image_sem)
     waits += filtered_steps + image_steps
 
@@ -507,8 +532,8 @@
             pltpu.VMEM((size, 128), BF16),
             sem((2, 2 * steps)),
             sem((2, 1)),
-            sem((2, 15)),
-            sem((2, 15)),
+            sem((2, 16)),
+            sem((2, 16)),
             sem((2, 4)),
             sem((2, 3)),
             sem((2, 7)),

time: 166 us -> 153 us (0.922)
  Pallas kernels: 160 us -> 148 us
    pallas_call x1, Pallas kernels: 157 us -> 144 us  [body(): pl.pallas_call(functools.partial(step_kernel, (cells, npc, owned, share,...]
where the time goes in v3:
time: 153 us
  Pallas kernels  148 us (97%)
  local copies, waits for them, and re-layouts  4.52 us (3%)
    pallas_call x1, Pallas kernels, body(): pl.pallas_call(functools.partial(step_kernel, (cells, npc, owned, share,...  144 us
    pallas_call x1, Pallas kernels, body(): pl.pallas_call(residual_kernel, out_shape=(jax.ShapeDtypeStruct((share, o...  3.59 us
    unnamed x1, local copies, waits for them, and re-layouts  3.21 us

profile of v3, /device:TPU:1, one launch (start us, length us, event | category | flops | bytes accessed | tf_op | source)
XLA Modules:
  0.0 153.1 jit_solution(6570079270445734635)
XLA Ops:
  0.6 1.3 broadcast_in_dim.6.pot_ref
  1.9 3.2 %copy.7.mats_ref = bf16[8,343,343]{2,1,0:T(8,128)(2,1)} copy(bf16[8,343,343]{2,0,1:T(8,128)(2,1)} %param.7) | data formatting | bytes 3764768 | tf_op args[2]
  5.2 144.4 %filter_and_project.1 = (bf16[160,1024]{1,0:T(8,128)(2,1)}, bf16[160,1024]{1,0:T(8,128)(2,1)}, bf16[5120,128]{1,0:T(8,128)(2,1)}) custom-call(bf16[64,2352]{1,0:T(8,128)(2,1)} %bitcast.2, f32[1,2352]{1,0:T(1,128)} %broadcast_in_dim.6.pot_ref, bf16[8,343,343]{2,1,0:T(8,128)(2,1)} %copy.7.mats_ref, s32[8,343]{1,0:T(8,128)} %conn_ref.1, s32[1,49]{1,0:T(1,128)} %bitcast.3), custom_call_target="tpu_custom_call" | custom-call | tf_op jit(solution)/shard_map/filter_and_project/pallas_call | solution.py:498
  149.5 3.6 %residual.1 = (f32[147,1024]{1,0:T(8,128)}, bf16[1024,1024]{1,0:T(8,128)(2,1)}) custom-call(bf16[160,1024]{1,0:T(8,128)(2,1)} %get-tuple-element.5.left_ref, bf16[160,1024]{1,0:T(8,128)(2,1)} %get-tuple-element.6.right_ref, bf16[5120,128]{1,0:T(8,128)(2,1)} %get-tuple-element.7.sum_ref), custom_call_target="tpu_custom_call" | custom-call | tf_op jit(solution)/shard_map/residual/pallas_call | solution.py:551

commit v4 on v3

--- a/solution.py
+++ b/solution.py
@@ -135,7 +135,7 @@
         pl.semaphore_signal(barrier, inc=1, device_id=peer, device_id_type=MESH)
 
     width = values.shape[2]
-    pot = pot_ref[...]
+    pot = pot_ref[...][None, :]
     upper = pot.astype(BF16)
     rest = pot - upper.astype(F32)
     middle = rest.astype(BF16)
@@ -357,15 +357,29 @@
 
     count = left_ref.shape[1] // BLOCK
     pairs = [(i, j) for i in range(count) for j in range(i, count)]
-    for p, (i, j) in enumerate(pairs):
-        block = lax.dot_general(
-            left_ref[:, i * BLOCK : (i + 1) * BLOCK],
-            right_ref[:, j * BLOCK : (j + 1) * BLOCK],
-            (((0,), (0,)), ((), ())),
-            preferred_element_type=F32,
-        ).astype(BF16)
-        packed[pl.ds((2 * p) * BLOCK, BLOCK), :] = block[:, :128]
-        packed[pl.ds((2 * p + 1) * BLOCK, BLOCK), :] = block[:, 128:]
+
+    def multiply(first, last):
+        for p in range(first, last):
+            i, j = pairs[p]
+            block = lax.dot_general(
+                left_ref[:, i * BLOCK : (i + 1) * BLOCK],
+                right_ref[:, j * BLOCK : (j + 1) * BLOCK],
+                (((0,), (0,)), ((), ())),
+                preferred_element_type=F32,
+            ).astype(BF16)
+            packed[pl.ds((2 * p) * BLOCK, BLOCK), :] = block[:, :128]
+            packed[pl.ds((2 * p + 1) * BLOCK, BLOCK), :] = block[:, 128:]
+
+    half_way = len(pairs) // 2
+
+    @pl.when(core == 0)
+    def _():
+        multiply(half_way, len(pairs))
+
+    @pl.when(core == 1)
+    def _():
+        multiply(0, half_way)
+
     size = packed.shape[0]
     n2, n8, n64, n1024 = size // 2, size // 8, size // 64, size // 1024
 
@@ -379,6 +393,15 @@
         steps[k] = copy(packed.at[at(piece, n8)], from_core.at[k], core_sem, k, at_core())
         steps[k].start()
     waits += [steps[k] for k in order]
+
+    @pl.when(core == 0)
+    def _():
+        multiply(0, half_way)
+
+    @pl.when(core == 1)
+    def _():
+        multiply(half_way, len(pairs))
+
     x_steps = {}
     for k in order:
         steps[k].wait_recv()
@@ -547,7 +570,7 @@
             collective_id=0, has_side_effects=True, vmem_limit_bytes=60 << 20
         ),
         name="filter_and_project",
-    )(orbitals.T, potential[None, :], cell_hamiltonian, connectivity, face_nodes[None, :])
+    )(orbitals.T, potential, cell_hamiltonian, connectivity, face_nodes[None, :])
     return pl.pallas_call(
         residual_kernel,
         out_shape=(

time: 153 us -> 150 us (0.980)
  Pallas kernels: 148 us -> 146 us
    pallas_call x1, Pallas kernels: 144 us -> 142 us  [body(): pl.pallas_call(functools.partial(step_kernel, (cells, npc, owned, share,...]
where the time goes in v4:
time: 150 us
  Pallas kernels  146 us (97%)
  local copies, waits for them, and re-layouts  3.21 us (2%)
    pallas_call x1, Pallas kernels, body(): pl.pallas_call(functools.partial(step_kernel, (cells, npc, owned, share,...  142 us
    pallas_call x1, Pallas kernels, body(): pl.pallas_call(residual_kernel, out_shape=(jax.ShapeDtypeStruct((share, o...  3.59 us
    unnamed x1, local copies, waits for them, and re-layouts  3.21 us

profile of v4, /device:TPU:1, one launch (start us, length us, event | category | flops | bytes accessed | tf_op | source)
XLA Modules:
  0.0 149.5 jit_solution(16055836893716411409)
XLA Ops:
  0.6 3.2 %copy.7.mats_ref = bf16[8,343,343]{2,1,0:T(8,128)(2,1)} copy(bf16[8,343,343]{2,0,1:T(8,128)(2,1)} %param.7) | data formatting | bytes 3764768 | tf_op args[2]
  3.8 142.1 %filter_and_project.1 = (bf16[160,1024]{1,0:T(8,128)(2,1)}, bf16[160,1024]{1,0:T(8,128)(2,1)}, bf16[5120,128]{1,0:T(8,128)(2,1)}) custom-call(bf16[64,2352]{1,0:T(8,128)(2,1)} %bitcast.2, f32[2352]{0:T(1024)} %pot_ref.1, bf16[8,343,343]{2,1,0:T(8,128)(2,1)} %copy.7.mats_ref, s32[8,343]{1,0:T(8,128)} %conn_ref.1, s32[1,49]{1,0:T(1,128)} %bitcast.3), custom_call_target="tpu_custom_call" | custom-call | tf_op jit(solution)/shard_map/filter_and_project/pallas_call | solution.py:521
  145.9 3.6 %residual.1 = (f32[147,1024]{1,0:T(8,128)}, bf16[1024,1024]{1,0:T(8,128)(2,1)}) custom-call(bf16[160,1024]{1,0:T(8,128)(2,1)} %get-tuple-element.5.left_ref, bf16[160,1024]{1,0:T(8,128)(2,1)} %get-tuple-element.6.right_ref, bf16[5120,128]{1,0:T(8,128)(2,1)} %get-tuple-element.7.sum_ref), custom_call_target="tpu_custom_call" | custom-call | tf_op jit(solution)/shard_map/residual/pallas_call | solution.py:574
